TPU v7x, 256 devices: a whole 4x4x8 slice. The times are simulated.
256 devices in a mesh: leaf: 16 (over x, y), rows: 16 (over z, core).
Axes of the slice: x: 4, y: 4, z: 8, core: 2. Of those that a mesh axis runs over, the one named last changes fastest.
Arguments:
- rhs_top: float32 [1, 4096, 128], P(None, 'rows'), may hold values from -6 to 6
- rhs_one: float32 [2, 2048, 128], P(None, 'rows'), may hold values from -6 to 6
- rhs_two: float32 [4, 2048, 128], P(None, 'rows'), may hold values from -6 to 6
- rhs_three: float32 [8, 1024, 128], P(None, 'rows'), may hold values from -6 to 6
- inv_top: float32 [4096, 4096], P('rows', 'leaf')
- inv_one: float32 [2048, 4096], P('rows', 'leaf')
- inv_two: float32 [2048, 8192], P('rows', 'leaf')
- inv_three: float32 [1024, 8192], P('rows', 'leaf')
- panel_one: float32 [4096, 2048], P('leaf', 'rows'), may hold values from -0.0625 to 0.0625
- panel_two: float32 [8192, 4096], P('leaf', 'rows'), may hold values from -0.0625 to 0.0625
- panel_three: float32 [8192, 4096], P('leaf', 'rows'), may hold values from -0.09375 to 0.09375
- rows_one: int32 [2, 16], P(None, 'rows'), may hold values from 0 to 31, as said below
- rows_two: int32 [4, 32], P(None, 'rows'), may hold values from 0 to 47, as said below
- rows_three: int32 [8, 32], P(None, 'rows'), may hold values from 0 to 63, as said below
Outputs:
- solution_top: float32 [1, 4096, 128], P(None, 'rows')
- solution_one: float32 [2, 2048, 128], P(None, 'rows')
- solution_two: float32 [4, 2048, 128], P(None, 'rows')
- solution_three: float32 [8, 1024, 128], P(None, 'rows')
Inputs may be any that keep to these rules, and one draw needn't show every extreme that they name: `rows_one`: each row lists 16 different blocks of a chain of 32 blocks, the chain's first and last among them. `rows_two`: each row lists 32 different blocks of a chain of 48 blocks, the chain's first and last among them. `rows_three`: each row lists 32 different blocks of a chain of 64 blocks, the chain's first and last among them.
All inputs are finite; a program needn't handle non-finite values.
Results may differ from a plain program's by a relative error of at most 0.0001.
Values sent between devices are 32-bit elements; how exact they have to be, the bound alone decides.
A program may use at most 64 MiB of HBM per device.

v0:
```python
import jax
import jax.numpy as jnp
from jax import lax
from jax.sharding import PartitionSpec as P

SEP0 = 4096
SEP1 = 2048
SEP2 = 2048
SEP3 = 1024
BLOCK = 128


def layout(sep_count, sep_size):
    span_rows = sep_count * sep_size // lax.axis_size("leaf")
    held_count = max(1, span_rows // sep_size)
    part_rows = min(span_rows, sep_size)
    first_sep = lax.axis_index("leaf") * span_rows // sep_size
    return (held_count, part_rows, first_sep)


def forward_solve(inverse, source, sep_count, sep_size):
    held_count, part_rows, first_sep = layout(sep_count, sep_size)
    picked = lax.dynamic_slice_in_dim(source, first_sep, held_count, 0)
    blocks = inverse.reshape(inverse.shape[0], held_count, part_rows)
    partial_y = jnp.einsum("csr,scn->srn", blocks, picked, precision=lax.Precision.HIGHEST)
    return lax.psum(partial_y, "rows")


def chain_matches(index_rows, first_sep, held_count, chain_count, listed):
    picked_rows = lax.dynamic_slice_in_dim(index_rows, first_sep, held_count, 0)
    column_ids = lax.broadcasted_iota(jnp.int32, (held_count, chain_count, listed), 1)
    return (column_ids == picked_rows[:, None, :]).astype(jnp.float32)


def ancestor_terms(panel, index_rows, solved_rows, sep_sizes, sep_counts, level_at):
    held_count, part_rows, first_sep = layout(sep_counts[level_at], sep_sizes[level_at])
    width_rhs = solved_rows.shape[2]
    listed = panel.shape[1] // BLOCK
    chain_count = sum(sep_sizes[:level_at]) // BLOCK
    panel_cut = panel.reshape(held_count, part_rows, listed * BLOCK)
    updates = jnp.einsum("sra,srn->san", panel_cut, solved_rows, precision=lax.Precision.HIGHEST)
    matches = chain_matches(index_rows, first_sep, held_count, chain_count, listed)
    spread = jnp.einsum(
        "sck,skbn->scbn",
        matches,
        updates.reshape(held_count, listed, BLOCK, width_rhs),
        precision=lax.Precision.HIGHEST,
    )
    owners = first_sep + jnp.arange(held_count, dtype=jnp.int32)
    results = []
    offset = 0
    for upper in range(level_at):
        blocks_up = sep_sizes[upper] // BLOCK
        segment = spread[:, offset : offset + blocks_up].reshape(
            held_count, sep_sizes[upper], width_rhs
        )
        target_ids = lax.broadcasted_iota(jnp.int32, (held_count, sep_counts[upper]), 1)
        target = (target_ids == (owners >> level_at - upper)[:, None]).astype(jnp.float32)
        results.append(jnp.einsum("sq,srn->qrn", target, segment, precision=lax.Precision.HIGHEST))
        offset = offset + blocks_up
    return results


def reduce_dense(parts):
    column_parts = lax.psum_scatter(parts, "rows", scatter_dimension=1, tiled=True)
    return lax.psum(column_parts, "leaf")


def backward_panel(panel, index_rows, gathered, solved_rows, sep_sizes, sep_counts, level_at):
    held_count, part_rows, first_sep = layout(sep_counts[level_at], sep_sizes[level_at])
    width_rhs = solved_rows.shape[2]
    listed = panel.shape[1] // BLOCK
    chain_count = sum(sep_sizes[:level_at]) // BLOCK
    owners = first_sep + jnp.arange(held_count, dtype=jnp.int32)
    pieces = []
    for upper in range(level_at):
        target_ids = lax.broadcasted_iota(jnp.int32, (held_count, sep_counts[upper]), 1)
        target = (target_ids == (owners >> level_at - upper)[:, None]).astype(jnp.float32)
        pieces.append(
            jnp.einsum("sq,qrn->srn", target, gathered[upper], precision=lax.Precision.HIGHEST)
        )
    chain_x = jnp.concatenate(pieces, axis=1).reshape(held_count, chain_count, BLOCK, width_rhs)
    matches = chain_matches(index_rows, first_sep, held_count, chain_count, listed)
    chosen = jnp.einsum("sck,scbn->skbn", matches, chain_x, precision=lax.Precision.HIGHEST)
    panel_cut = panel.reshape(held_count, part_rows, listed * BLOCK)
    partial_g = jnp.einsum(
        "sra,san->srn",
        panel_cut,
        chosen.reshape(held_count, listed * BLOCK, width_rhs),
        precision=lax.Precision.HIGHEST,
    )
    return solved_rows - lax.psum(partial_g, "rows")


def backward_solve(inverse, residue, sep_count, sep_size):
    held_count, part_rows, first_sep = layout(sep_count, sep_size)
    blocks = inverse.reshape(inverse.shape[0], held_count, part_rows)
    partial_x = jnp.einsum("csr,srn->scn", blocks, residue, precision=lax.Precision.HIGHEST)
    owners = first_sep + jnp.arange(held_count, dtype=jnp.int32)
    place_ids = lax.broadcasted_iota(jnp.int32, (held_count, sep_count), 1)
    placing = (place_ids == owners[:, None]).astype(jnp.float32)
    dense = jnp.einsum("sq,scn->qcn", placing, partial_x, precision=lax.Precision.HIGHEST)
    return lax.psum(dense, "leaf")


def body(
    rhs_top,
    rhs_one,
    rhs_two,
    rhs_three,
    inv_top,
    inv_one,
    inv_two,
    inv_three,
    panel_one,
    panel_two,
    panel_three,
    rows_one,
    rows_two,
    rows_three,
):
    sep_sizes = [SEP0, SEP1, SEP2, SEP3]
    sep_counts = [1, 2, 4, 8]
    right_sides = [rhs_top, rhs_one, rhs_two, rhs_three]
    inverses = [inv_top, inv_one, inv_two, inv_three]
    panels = [None, panel_one, panel_two, panel_three]
    indices = [None, rows_one, rows_two, rows_three]
    solved = [None, None, None, None]
    owed_rows = [jnp.zeros(item.shape, jnp.float32) for item in right_sides]
    for level_at in (3, 2, 1, 0):
        source = right_sides[level_at] - owed_rows[level_at]
        solved[level_at] = forward_solve(
            inverses[level_at], source, sep_counts[level_at], sep_sizes[level_at]
        )
        if level_at > 0:
            fresh = ancestor_terms(
                panels[level_at],
                indices[level_at],
                solved[level_at],
                sep_sizes,
                sep_counts,
                level_at,
            )
            reduced = reduce_dense(tuple(fresh))
            for upper in range(level_at):
                owed_rows[upper] = owed_rows[upper] + reduced[upper]
    gathered = []
    results = []
    for level_at in range(4):
        residue = solved[level_at]
        if level_at > 0:
            residue = backward_panel(
                panels[level_at],
                indices[level_at],
                gathered,
                solved[level_at],
                sep_sizes,
                sep_counts,
                level_at,
            )
        solution_cols = backward_solve(
            inverses[level_at], residue, sep_counts[level_at], sep_sizes[level_at]
        )
        results.append(solution_cols)
        if level_at < 3:
            gathered.append(lax.all_gather(solution_cols, "rows", axis=1, tiled=True))
    return (results[0], results[1], results[2], results[3])


def solution(mesh):
    return jax.shard_map(
        body,
        mesh=mesh,
        in_specs=(
            P(None, "rows", None),
            P(None, "rows", None),
            P(None, "rows", None),
            P(None, "rows", None),
            P("rows", "leaf"),
            P("rows", "leaf"),
            P("rows", "leaf"),
            P("rows", "leaf"),
            P("leaf", "rows"),
            P("leaf", "rows"),
            P("leaf", "rows"),
            P(None, "rows"),
            P(None, "rows"),
            P(None, "rows"),
        ),
        out_specs=(
            P(None, "rows", None),
            P(None, "rows", None),
            P(None, "rows", None),
            P(None, "rows", None),
        ),
        check_vma=False,
    )
```

profile of v0, /device:TPU:2, one launch (start us, length us, event | category | flops | bytes accessed | tf_op | source)
XLA Modules:
  0.0 1859.5 jit_solution(8080732922114036708)
XLA Ops:
  7.2 2.1 convolution_bitcast_fusion.5
  9.4 0.9 fusion.41
  10.3 113.3 %all-reduce.15.cloned.1.call-done = f32[1,512,128]{1,2,0:T(8,128)} async-done(((f32[1,512,128]{1,2,0:T(8,128)}), f32[1,512,128]{1,2,0:T(8,128)}) %all-reduce.15.cloned.1.call-update) | async-done | bytes 262160 | tf_op jit(solution)/shard_map/psum | solution.py:26
  123.6 1.5 convolution_bitcast_fusion.8
  125.4 1.9 convolution_bitcast_fusion
  127.5 1.8 copy-done.1
  129.6 2.3 broadcast_multiply_fusion
  132.0 63.9 %reduce-scatter.4.cloned.1.call-done = f32[4,128,128]{2,1,0:T(8,128)} async-done(((f32[4,2048,128]{2,1,0:T(8,128)}), f32[4,128,128]{2,1,0:T(8,128)}) %reduce-scatter.4.cloned.1.call-update) | async-done | bytes 262160 | tf_op jit(solution)/shard_map/reduce_scatter | solution.py:65
  196.0 96.3 %all-reduce.17.cloned.1.call-done = f32[4,128,128]{2,1,0:T(8,128)} async-done(((f32[4,128,128]{2,1,0:T(8,128)}), f32[4,128,128]{2,1,0:T(8,128)}) %all-reduce.17.cloned.1.call-update) | async-done | bytes 262160 | tf_op jit(solution)/shard_map/psum | solution.py:66
  292.3 2.0 convolution_bitcast_fusion.4
  294.9 109.9 %all-reduce.19.cloned.1.call-done = f32[1,512,128]{1,2,0:T(8,128)} async-done(((f32[1,512,128]{1,2,0:T(8,128)}), f32[1,512,128]{1,2,0:T(8,128)}) %all-reduce.19.cloned.1.call-update) | async-done | bytes 262160 | tf_op jit(solution)/shard_map/psum | solution.py:26
  404.8 1.3 convolution_bitcast_fusion.7
  406.4 1.5 convolution_bitcast_fusion.1
  408.3 1.2 copy-done.2
  409.6 1.7 multiply_add_fusion
  411.4 60.6 %reduce-scatter.6.cloned.1.call-done = f32[2,128,128]{2,1,0:T(8,128)} async-done(((f32[2,2048,128]{2,1,0:T(8,128)}), f32[2,128,128]{2,1,0:T(8,128)}) %reduce-scatter.6.cloned.1.call-update) | async-done | bytes 131088 | tf_op jit(solution)/shard_map/reduce_scatter | solution.py:65
  473.3 93.1 %all-reduce.39.cloned.1.call-done = f32[2,128,128]{2,1,0:T(8,128)} async-done(((f32[2,128,128]{2,1,0:T(8,128)}), f32[2,128,128]{2,1,0:T(8,128)}) %all-reduce.39.cloned.1.call-update) | async-done | bytes 131088 | tf_op jit(solution)/shard_map/psum | solution.py:66
  566.4 1.8 convolution_bitcast_fusion.10
  568.3 2.8 fusion.2
  571.0 1.2 copy.29
  572.3 106.2 %all-reduce.21.cloned.1.call-done = f32[1,256,128]{1,2,0:T(8,128)} async-done(((f32[1,256,128]{1,2,0:T(8,128)}), f32[1,256,128]{1,2,0:T(8,128)}) %all-reduce.21.cloned.1.call-update) | async-done | bytes 131088 | tf_op jit(solution)/shard_map/psum | solution.py:26
  678.5 1.2 convolution_bitcast_fusion.12
  680.0 1.6 bitcast_add_fusion
  681.7 60.9 %reduce-scatter.8.cloned.1.call-done = f32[1,256,128]{2,1,0:T(8,128)} async-done(((f32[1,4096,128]{2,1,0:T(8,128)}), f32[1,256,128]{2,1,0:T(8,128)}) %reduce-scatter.8.cloned.1.call-update) | async-done | bytes 131088 | tf_op jit(solution)/shard_map/reduce_scatter | solution.py:65
  742.6 94.3 %all-reduce.41.cloned.1.call-done = f32[1,256,128]{2,1,0:T(8,128)} async-done(((f32[1,256,128]{2,1,0:T(8,128)}), f32[1,256,128]{2,1,0:T(8,128)}) %all-reduce.41.cloned.1.call-update) | async-done | bytes 131088 | tf_op jit(solution)/shard_map/psum | solution.py:66
  837.0 2.0 convolution_bitcast_fusion.6
  839.0 109.9 %all-reduce.23.cloned.1.call-done = f32[256,128]{0,1:T(8,128)} async-done(((f32[256,128]{0,1:T(8,128)}), f32[256,128]{0,1:T(8,128)}) %all-reduce.23.cloned.1.call-update) | async-done | bytes 131088 | tf_op jit(solution)/shard_map/psum | solution.py:26
  948.9 2.0 fusion.7
  951.0 95.2 %all-reduce.25.cloned.1.call-done = f32[1,256,128]{1,2,0:T(8,128)} async-done(((f32[1,256,128]{1,2,0:T(8,128)}), f32[1,256,128]{1,2,0:T(8,128)}) %all-reduce.25.cloned.1.call-update) | async-done | bytes 131088 | tf_op jit(solution)/shard_map/psum | solution.py:103
  1046.4 40.7 %all-gather.4.cloned.1.call-done = f32[1,4096,128]{1,2,0:T(8,128)} async-done(((f32[1,256,128]{1,2,0:T(8,128)}), f32[1,4096,128]{1,2,0:T(8,128)}) %all-gather.4.cloned.1.call-update) | async-done | bytes 2097168 | tf_op jit(solution)/shard_map/all_gather | solution.py:166
  1087.2 3.7 broadcast_multiply_fusion.1
  1091.3 1.5 fusion.31
  1092.7 0.9 convolution_bitcast_fusion.9
  1093.8 107.9 %all-reduce.27.cloned.1.call-done = f32[1,256,128]{1,2,0:T(8,128)} async-done(((f32[1,256,128]{1,2,0:T(8,128)}), f32[1,256,128]{1,2,0:T(8,128)}) %all-reduce.27.cloned.1.call-update) | async-done | bytes 131088 | tf_op jit(solution)/shard_map/psum | solution.py:92
  1201.6 1.2 convolution_bitcast_fusion.11
  1203.7 95.0 %all-reduce.29.cloned.1.call-done = f32[2,128,128]{2,1,0:T(8,128)} async-done(((f32[2,128,128]{2,1,0:T(8,128)}), f32[2,128,128]{2,1,0:T(8,128)}) %all-reduce.29.cloned.1.call-update) | async-done | bytes 131088 | tf_op jit(solution)/shard_map/psum | solution.py:103
  1298.8 40.9 %all-gather.6.cloned.1.call-done = f32[2,2048,128]{2,1,0:T(8,128)} async-done(((f32[2,128,128]{2,1,0:T(8,128)}), f32[2,2048,128]{2,1,0:T(8,128)}) %all-gather.6.cloned.1.call-update) | async-done | bytes 2097168 | tf_op jit(solution)/shard_map/all_gather | solution.py:166
  1339.7 7.6 fusion.5
  1347.3 3.6 copy.42
  1350.9 1.5 maximum_bitcast_fusion.1
  1352.4 2.2 copy.47
  1354.5 3.6 copy.34
  1358.1 3.0 fusion.33
  1361.2 1.4 convolution_bitcast_fusion.3
  1362.7 108.2 %all-reduce.31.cloned.1.call-done = f32[1,512,128]{1,2,0:T(8,128)} async-done(((f32[1,512,128]{1,2,0:T(8,128)}), f32[1,512,128]{1,2,0:T(8,128)}) %all-reduce.31.cloned.1.call-update) | async-done | bytes 262160 | tf_op jit(solution)/shard_map/psum | solution.py:92
  1470.9 1.3 convolution_bitcast_fusion.13
  1472.3 0.8 broadcast_multiply_fusion.4
  1473.2 96.5 %all-reduce.33.cloned.1.call-done = f32[4,128,128]{2,1,0:T(8,128)} async-done(((f32[4,128,128]{2,1,0:T(8,128)}), f32[4,128,128]{2,1,0:T(8,128)}) %all-reduce.33.cloned.1.call-update) | async-done | bytes 262160 | tf_op jit(solution)/shard_map/psum | solution.py:103
  1570.0 6.6 fusion.3
  1576.6 1.9 copy.43
  1578.5 34.7 %all-gather.8.cloned.1.call-done = f32[4,2048,128]{2,1,0:T(8,128)} async-done(((f32[4,128,128]{2,1,0:T(8,128)}), f32[4,2048,128]{2,1,0:T(8,128)}) %all-gather.8.cloned.1.call-update) | async-done | bytes 4194320 | tf_op jit(solution)/shard_map/all_gather | solution.py:166
  1613.1 9.6 fusion
  1622.7 3.8 copy.45
  1626.6 1.9 maximum_bitcast_fusion
  1628.4 2.7 copy.48
  1631.1 5.5 copy.37
  1636.6 3.7 fusion.36
  1640.4 1.4 convolution_bitcast_fusion.2
  1641.9 108.6 %all-reduce.35.cloned.1.call-done = f32[1,512,128]{1,2,0:T(8,128)} async-done(((f32[1,512,128]{1,2,0:T(8,128)}), f32[1,512,128]{1,2,0:T(8,128)}) %all-reduce.35.cloned.1.call-update) | async-done | bytes 262160 | tf_op jit(solution)/shard_map/psum | solution.py:92
  1750.5 1.3 convolution_bitcast_fusion.14
  1751.8 0.8 broadcast_multiply_fusion.3
  1752.7 0.8 copy.39
  1753.4 95.9 %all-reduce.37.cloned.1.call-done = f32[8,64,128]{2,1,0:T(8,128)} async-done(((f32[8,64,128]{2,1,0:T(8,128)}), f32[8,64,128]{2,1,0:T(8,128)}) %all-reduce.37.cloned.1.call-update) | async-done | bytes 262160 | tf_op jit(solution)/shard_map/psum | solution.py:103
  1850.7 1.7 copy.71
  (106 shorter events, 7.7 us)
Async XLA Ops:
  7.2 397.6 %copy-start = (f32[512,256]{1,0:T(8,128)S(1)}, f32[512,256]{1,0:T(8,128)}, u32[]{:S(2)}) copy-start(f32[512,256]{1,0:T(8,128)} %param.23) | copy-start | bytes 1572868
  7.2 116.4 %all-reduce.15.cloned.1.call-start = ((), (), s32[]{:S(2)}) async-start(), calls=%async_computation.3 | async-start | bytes 524288 | tf_op jit(solution)/shard_map/psum | solution.py:26
  9.4 186.5 %reduce-scatter.4.cloned.1.call-start = ((), (), s32[]{:S(2)}) async-start(), calls=%async_computation.4 | async-start | bytes 4456448 | tf_op jit(solution)/shard_map/reduce_scatter | solution.py:65
  127.3 1.9 copy-start.1
  131.9 160.4 %copy-start.8 = (f32[128,512]{1,0:T(8,128)S(1)}, f32[128,512]{1,0:T(8,128)}, u32[]{:S(2)}) copy-start(f32[128,512]{1,0:T(8,128)} %param.20) | copy-start | bytes 786436
  131.9 162.4 %copy-start.18 = (s32[4,2]{0,1:T(2,128)S(1)}, s32[4,2]{0,1:T(2,128)}, u32[]{:S(2)}) copy-start(s32[4,2]{0,1:T(2,128)} %param.26) | copy-start | bytes 100
  132.0 160.3 %all-reduce.17.cloned.1.call-start = ((), (), s32[]{:S(2)}) async-start(), calls=%async_computation.5 | async-start | bytes 524288 | tf_op jit(solution)/shard_map/psum | solution.py:66
  195.9 208.9 %all-reduce.19.cloned.1.call-start = ((), (), s32[]{:S(2)}) async-start(), calls=%async_computation.6 | async-start | bytes 524288 | tf_op jit(solution)/shard_map/psum | solution.py:26
  294.3 177.6 %reduce-scatter.6.cloned.1.call-start = ((), (), s32[]{:S(2)}) async-start(), calls=%async_computation.21 | async-start | bytes 2228224 | tf_op jit(solution)/shard_map/reduce_scatter | solution.py:65
  407.9 1.7 copy-start.2
  411.3 60.8 %copy-start.19 = (s32[2,1]{0,1:T(1,128)S(1)}, s32[2,1]{0,1:T(1,128)}, u32[]{:S(2)}) copy-start(s32[2,1]{0,1:T(1,128)} %param.25) | copy-start | bytes 28
  411.3 155.1 %copy-start.10 = (f32[128,256]{1,0:T(8,128)S(1)}, f32[128,256]{1,0:T(8,128)}, u32[]{:S(2)}) copy-start(f32[128,256]{1,0:T(8,128)} %param.19) | copy-start | bytes 393220
  411.3 155.1 %copy-start.17 = (f32[2,128,128]{2,1,0:T(8,128)S(1)}, f32[2,128,128]{2,1,0:T(8,128)}, u32[]{:S(2)}) copy-start(f32[2,128,128]{2,1,0:T(8,128)} %param.15) | copy-start | bytes 393220
  411.3 155.1 %all-reduce.39.cloned.1.call-start = ((), (), s32[]{:S(2)}) async-start(), calls=%async_computation.19 | async-start | bytes 262144 | tf_op jit(solution)/shard_map/psum | solution.py:66
  472.0 206.5 %all-reduce.21.cloned.1.call-start = ((), (), s32[]{:S(2)}) async-start(), calls=%async_computation.7 | async-start | bytes 262144 | tf_op jit(solution)/shard_map/psum | solution.py:26
  568.2 174.4 %reduce-scatter.8.cloned.1.call-start = ((), (), s32[]{:S(2)}) async-start(), calls=%async_computation.22 | async-start | bytes 2228224 | tf_op jit(solution)/shard_map/reduce_scatter | solution.py:65
  571.0 107.5 %copy-start.12 = (f32[256,128]{1,0:T(8,128)S(1)}, f32[256,128]{1,0:T(8,128)}, u32[]{:S(2)}) copy-start(f32[256,128]{1,0:T(8,128)} %param.22) | copy-start | bytes 393220
  681.6 155.3 %copy-start.7 = (f32[256,256]{1,0:T(8,128)S(1)}, f32[256,256]{1,0:T(8,128)}, u32[]{:S(2)}) copy-start(f32[256,256]{1,0:T(8,128)} %param.18) | copy-start | bytes 786436
  681.6 155.3 %copy-start.16 = (f32[1,256,128]{2,1,0:T(8,128)S(1)}, f32[1,256,128]{2,1,0:T(8,128)}, u32[]{:S(2)}) copy-start(f32[1,256,128]{2,1,0:T(8,128)} %param.14) | copy-start | bytes 393220
  681.7 155.3 %all-reduce.41.cloned.1.call-start = ((), (), s32[]{:S(2)}) async-start(), calls=%async_computation.20 | async-start | bytes 262144 | tf_op jit(solution)/shard_map/psum | solution.py:66
  742.6 206.3 %all-reduce.23.cloned.1.call-start = ((), (), s32[]{:S(2)}) async-start(), calls=%async_computation.8 | async-start | bytes 262144 | tf_op jit(solution)/shard_map/psum | solution.py:26
  838.9 207.2 %all-reduce.25.cloned.1.call-start = ((), (), s32[]{:S(2)}) async-start(), calls=%async_computation.9 | async-start | bytes 262144 | tf_op jit(solution)/shard_map/psum | solution.py:103
  950.9 136.2 %all-gather.4.cloned.1.call-start = ((), (), s32[]{:S(2)}) async-start(), calls=%async_computation.10 | async-start | bytes 2228224 | tf_op jit(solution)/shard_map/all_gather | solution.py:166
  1046.2 155.4 %all-reduce.27.cloned.1.call-start = ((), (), s32[]{:S(2)}) async-start(), calls=%async_computation.11 | async-start | bytes 262144 | tf_op jit(solution)/shard_map/psum | solution.py:92
  1091.2 110.4 %copy-start.11 = (f32[1,256,128]{1,2,0:T(8,128)S(1)}, f32[1,256,128]{1,2,0:T(8,128)}, u32[]{:S(2)}) copy-start(f32[1,256,128]{1,2,0:T(8,128)} %all-reduce.21.cloned.1.call-done) | copy-start | bytes 393220
  1093.7 205.0 %all-reduce.29.cloned.1.call-start = ((), (), s32[]{:S(2)}) async-start(), calls=%async_computation.12 | async-start | bytes 262144 | tf_op jit(solution)/shard_map/psum | solution.py:103
  1203.7 136.0 %all-gather.6.cloned.1.call-start = ((), (), s32[]{:S(2)}) async-start(), calls=%async_computation.13 | async-start | bytes 2228224 | tf_op jit(solution)/shard_map/all_gather | solution.py:166
  1298.7 172.2 %all-reduce.31.cloned.1.call-start = ((), (), s32[]{:S(2)}) async-start(), calls=%async_computation.14 | async-start | bytes 524288 | tf_op jit(solution)/shard_map/psum | solution.py:92
  1358.1 112.8 %copy-start.6 = (f32[1,512,128]{1,2,0:T(8,128)S(1)}, f32[1,512,128]{1,2,0:T(8,128)}, u32[]{:S(2)}) copy-start(f32[1,512,128]{1,2,0:T(8,128)} %all-reduce.19.cloned.1.call-done) | copy-start | bytes 786436
  1362.6 207.1 %all-reduce.33.cloned.1.call-start = ((), (), s32[]{:S(2)}) async-start(), calls=%async_computation.15 | async-start | bytes 524288 | tf_op jit(solution)/shard_map/psum | solution.py:103
  1473.2 140.0 %all-gather.8.cloned.1.call-start = ((), (), s32[]{:S(2)}) async-start(), calls=%async_computation.16 | async-start | bytes 4456448 | tf_op jit(solution)/shard_map/all_gather | solution.py:166
  1569.7 180.7 %all-reduce.35.cloned.1.call-start = ((), (), s32[]{:S(2)}) async-start(), calls=%async_computation.17 | async-start | bytes 524288 | tf_op jit(solution)/shard_map/psum | solution.py:92
  1622.7 3.8 copy-start.3
  1636.6 3.8 copy-start.4
  1636.6 113.9 %copy-start.5 = (f32[1,512,128]{1,2,0:T(8,128)S(1)}, f32[1,512,128]{1,2,0:T(8,128)}, u32[]{:S(2)}) copy-start(f32[1,512,128]{1,2,0:T(8,128)} %all-reduce.15.cloned.1.call-done) | copy-start | bytes 786436
  1636.6 113.9 %copy-start.15 = (f32[64,512]{1,0:T(8,128)S(1)}, f32[64,512]{1,0:T(8,128)}, u32[]{:S(2)}) copy-start(f32[64,512]{1,0:T(8,128)} %param.21) | copy-start | bytes 393220
  1640.3 112.3 %copy-start.13 = (f32[1,256,128]{1,2,0:T(8,128)S(1)}, f32[1,256,128]{1,2,0:T(8,128)}, u32[]{:S(2)}) copy-start(f32[1,256,128]{1,2,0:T(8,128)} %all-reduce.25.cloned.1.call-done) | copy-start | bytes 393220
  1640.3 209.0 %copy-start.14 = (f32[2,128,128]{2,1,0:T(8,128)S(1)}, f32[2,128,128]{2,1,0:T(8,128)}, u32[]{:S(2)}) copy-start(f32[2,128,128]{2,1,0:T(8,128)} %all-reduce.29.cloned.1.call-done) | copy-start | bytes 393220
  1640.3 209.6 %copy-start.9 = (f32[4,128,128]{2,1,0:T(8,128)S(1)}, f32[4,128,128]{2,1,0:T(8,128)}, u32[]{:S(2)}) copy-start(f32[4,128,128]{2,1,0:T(8,128)} %all-reduce.33.cloned.1.call-done) | copy-start | bytes 786436
  1641.8 207.5 %all-reduce.37.cloned.1.call-start = ((), (), s32[]{:S(2)}) async-start(), calls=%async_computation.18 | async-start | bytes 524288 | tf_op jit(solution)/shard_map/psum | solution.py:103
Sparse Core Ops, SparseCore 0:
  10.9 112.7 all-reduce.14
  132.1 63.7 reduce-scatter.3
  199.0 93.1 all-reduce.16
  295.0 109.7 all-reduce.18
  411.4 60.4 reduce-scatter.5
  475.0 91.3 all-reduce.38
  569.3 109.2 all-reduce.20
  681.8 60.7 reduce-scatter.7
  745.8 91.1 all-reduce.40
  839.7 109.1 all-reduce.22
  952.7 93.4 all-reduce.24
  1047.9 39.2 all-gather.3
  1093.8 107.7 all-reduce.26
  1205.2 93.4 all-reduce.28
  1300.4 39.2 all-gather.5
  1362.7 108.1 all-reduce.30
  1474.5 95.1 all-reduce.32
  1571.4 41.6 all-gather.7
  1641.9 108.4 all-reduce.34
  1754.1 95.1 all-reduce.36
where the time goes:
time: 1870 us; the launch traced here: 1860 us
  waiting for transfers between devices  1730 us (93%)
  matrix products  56.9 us (3%)
  local copies, waits for them, and re-layouts  35.2 us (2%)
  other arithmetic  18.7 us (1%)
    psum x4, waiting for transfers between devices, forward_solve(): return lax.psum(partial_y, 'rows')  439 us
    psum x4, waiting for transfers between devices, backward_solve(): return lax.psum(dense, 'leaf')  383 us
    psum x3, waiting for transfers between devices, backward_panel(): return solved_rows - lax.psum(partial_g, 'rows')  325 us
    psum x3, waiting for transfers between devices, reduce_dense(): return lax.psum(column_parts, 'leaf')  284 us
    reduce_scatter x3, waiting for transfers between devices, reduce_dense(): lax.psum_scatter(parts, 'rows', scatter_dimension=1, tiled=True)  185 us
    all_gather x3, waiting for transfers between devices, body(): gathered.append(lax.all_gather(solution_cols, 'rows', axis=1, tiled=True))  116 us
  transfers between devices with their start and end apart: 20, of which 20 were waited for; matrix products, arithmetic and copies ran while one was open for 1% of the time, Pallas kernels for 0%

commit v1 on v0

--- a/solution.py
+++ b/solution.py
@@ -23,7 +23,7 @@
     picked = lax.dynamic_slice_in_dim(source, first_sep, held_count, 0)
     blocks = inverse.reshape(inverse.shape[0], held_count, part_rows)
     partial_y = jnp.einsum("csr,scn->srn", blocks, picked, precision=lax.Precision.HIGHEST)
-    return lax.psum(partial_y, "rows")
+    return jnp.sum(lax.all_gather(partial_y, "rows"), axis=0)
 
 
 def chain_matches(index_rows, first_sep, held_count, chain_count, listed):

time: 1870 us -> 1600 us (0.86)
  waiting for transfers between devices: 1730 us -> 1440 us
    psum x4 -> x0, waiting for transfers between devices: 439 us -> none  [forward_solve(): return lax.psum(partial_y, 'rows')]
    all_gather x0 -> x4, waiting for transfers between devices: none -> 160 us  [forward_solve(): return jnp.sum(lax.all_gather(partial_y, 'rows'), axis=0)]
where the time goes in v1:
time: 1600 us; the launch traced here: 1590 us
  waiting for transfers between devices  1440 us (90%)
  matrix products  54.2 us (3%)
  local copies, waits for them, and re-layouts  53.7 us (3%)
  other arithmetic  22 us (1%)
    psum x4, waiting for transfers between devices, backward_solve(): return lax.psum(dense, 'leaf')  377 us
    psum x3, waiting for transfers between devices, backward_panel(): return solved_rows - lax.psum(partial_g, 'rows')  325 us
    psum x3, waiting for transfers between devices, reduce_dense(): return lax.psum(column_parts, 'leaf')  285 us
    reduce_scatter x3, waiting for transfers between devices, reduce_dense(): lax.psum_scatter(parts, 'rows', scatter_dimension=1, tiled=True)  179 us
    all_gather x4, waiting for transfers between devices, forward_solve(): return jnp.sum(lax.all_gather(partial_y, 'rows'), axis=0)  160 us
    all_gather x3, waiting for transfers between devices, body(): gathered.append(lax.all_gather(solution_cols, 'rows', axis=1, tiled=True))  117 us
  transfers between devices with their start and end apart: 20, of which 20 were waited for; matrix products, arithmetic and copies ran while one was open for 1% of the time, Pallas kernels for 0%

profile of v1, /device:TPU:2, one launch (start us, length us, event | category | flops | bytes accessed | tf_op | source)
XLA Modules:
  0.0 1589.5 jit_solution(6960801663441611233)
XLA Ops:
  7.2 2.1 convolution_bitcast_fusion.5
  10.3 45.0 %all-gather.18.cloned.1.call-done = f32[8192,128]{0,1:T(8,128)} async-done(((f32[512,128]{0,1:T(8,128)}), f32[8192,128]{0,1:T(8,128)}) %all-gather.18.cloned.1.call-update) | async-done | bytes 4194320 | tf_op jit(solution)/shard_map/all_gather | solution.py:26
  55.3 5.4 copy.60
  62.4 1.9 convolution_bitcast_fusion
  64.5 1.8 copy-done.1
  66.6 2.3 broadcast_multiply_fusion
  69.0 62.1 %reduce-scatter.4.cloned.1.call-done = f32[4,128,128]{2,1,0:T(8,128)} async-done(((f32[4,2048,128]{2,1,0:T(8,128)}), f32[4,128,128]{2,1,0:T(8,128)}) %reduce-scatter.4.cloned.1.call-update) | async-done | bytes 262160 | tf_op jit(solution)/shard_map/reduce_scatter | solution.py:65
  131.2 96.1 %all-reduce.11.cloned.1.call-done = f32[4,128,128]{2,1,0:T(8,128)} async-done(((f32[4,128,128]{2,1,0:T(8,128)}), f32[4,128,128]{2,1,0:T(8,128)}) %all-reduce.11.cloned.1.call-update) | async-done | bytes 262160 | tf_op jit(solution)/shard_map/psum | solution.py:66
  227.4 2.0 convolution_bitcast_fusion.4
  230.2 41.2 %all-gather.20.cloned.1.call-done = f32[8192,128]{0,1:T(8,128)} async-done(((f32[512,128]{0,1:T(8,128)}), f32[8192,128]{0,1:T(8,128)}) %all-gather.20.cloned.1.call-update) | async-done | bytes 4194320 | tf_op jit(solution)/shard_map/all_gather | solution.py:26
  271.4 5.4 copy.61
  278.3 1.5 convolution_bitcast_fusion.1
  280.3 1.2 copy-done.2
  281.6 1.7 multiply_add_fusion
  283.3 58.6 %reduce-scatter.6.cloned.1.call-done = f32[2,128,128]{2,1,0:T(8,128)} async-done(((f32[2,2048,128]{2,1,0:T(8,128)}), f32[2,128,128]{2,1,0:T(8,128)}) %reduce-scatter.6.cloned.1.call-update) | async-done | bytes 131088 | tf_op jit(solution)/shard_map/reduce_scatter | solution.py:65
  342.1 94.3 %all-reduce.27.cloned.1.call-done = f32[2,128,128]{2,1,0:T(8,128)} async-done(((f32[2,128,128]{2,1,0:T(8,128)}), f32[2,128,128]{2,1,0:T(8,128)}) %all-reduce.27.cloned.1.call-update) | async-done | bytes 131088 | tf_op jit(solution)/shard_map/psum | solution.py:66
  436.4 1.8 convolution_bitcast_fusion.10
  439.5 2.8 fusion.2
  442.3 1.2 copy.43
  443.5 34.6 %all-gather.22.cloned.1.call-done = f32[4096,128]{0,1:T(8,128)} async-done(((f32[256,128]{0,1:T(8,128)}), f32[4096,128]{0,1:T(8,128)}) %all-gather.22.cloned.1.call-update) | async-done | bytes 2097168 | tf_op jit(solution)/shard_map/all_gather | solution.py:26
  478.1 2.3 copy.62
  482.1 1.6 copy.46
  483.7 1.1 multiply_multiply_fusion
  484.8 1.6 bitcast_add_fusion
  486.5 58.4 %reduce-scatter.8.cloned.1.call-done = f32[1,256,128]{2,1,0:T(8,128)} async-done(((f32[1,4096,128]{2,1,0:T(8,128)}), f32[1,256,128]{2,1,0:T(8,128)}) %reduce-scatter.8.cloned.1.call-update) | async-done | bytes 131088 | tf_op jit(solution)/shard_map/reduce_scatter | solution.py:65
  545.4 94.3 %all-reduce.29.cloned.1.call-done = f32[1,256,128]{2,1,0:T(8,128)} async-done(((f32[1,256,128]{2,1,0:T(8,128)}), f32[1,256,128]{2,1,0:T(8,128)}) %all-reduce.29.cloned.1.call-update) | async-done | bytes 131088 | tf_op jit(solution)/shard_map/psum | solution.py:66
  639.7 2.0 convolution_bitcast_fusion.6
  641.7 39.5 %all-gather.24.cloned.1.call-done = f32[4096,128]{0,1:T(8,128)} async-done(((f32[256,128]{0,1:T(8,128)}), f32[4096,128]{0,1:T(8,128)}) %all-gather.24.cloned.1.call-update) | async-done | bytes 2097168 | tf_op jit(solution)/shard_map/all_gather | solution.py:26
  681.3 2.3 copy.63
  683.9 1.1 fusion.7
  685.0 91.3 %all-reduce.13.cloned.1.call-done = f32[1,256,128]{1,2,0:T(8,128)} async-done(((f32[1,256,128]{1,2,0:T(8,128)}), f32[1,256,128]{1,2,0:T(8,128)}) %all-reduce.13.cloned.1.call-update) | async-done | bytes 131088 | tf_op jit(solution)/shard_map/psum | solution.py:103
  776.4 40.9 %all-gather.12.cloned.1.call-done = f32[1,4096,128]{1,2,0:T(8,128)} async-done(((f32[1,256,128]{1,2,0:T(8,128)}), f32[1,4096,128]{1,2,0:T(8,128)}) %all-gather.12.cloned.1.call-update) | async-done | bytes 2097168 | tf_op jit(solution)/shard_map/all_gather | solution.py:166
  817.3 3.7 broadcast_multiply_fusion.1
  821.4 1.5 fusion.25
  822.9 0.9 convolution_bitcast_fusion.9
  823.9 107.9 %all-reduce.15.cloned.1.call-done = f32[1,256,128]{1,2,0:T(8,128)} async-done(((f32[1,256,128]{1,2,0:T(8,128)}), f32[1,256,128]{1,2,0:T(8,128)}) %all-reduce.15.cloned.1.call-update) | async-done | bytes 131088 | tf_op jit(solution)/shard_map/psum | solution.py:92
  931.8 1.9 convolution_bitcast_fusion.11
  933.6 0.9 copy.47
  935.4 93.5 %all-reduce.17.cloned.1.call-done = f32[2,128,128]{2,1,0:T(8,128)} async-done(((f32[2,128,128]{2,1,0:T(8,128)}), f32[2,128,128]{2,1,0:T(8,128)}) %all-reduce.17.cloned.1.call-update) | async-done | bytes 131088 | tf_op jit(solution)/shard_map/psum | solution.py:103
  1029.0 40.9 %all-gather.14.cloned.1.call-done = f32[2,2048,128]{2,1,0:T(8,128)} async-done(((f32[2,128,128]{2,1,0:T(8,128)}), f32[2,2048,128]{2,1,0:T(8,128)}) %all-gather.14.cloned.1.call-update) | async-done | bytes 2097168 | tf_op jit(solution)/shard_map/all_gather | solution.py:166
  1069.9 7.5 fusion.5
  1077.4 3.6 copy.56
  1081.1 1.5 maximum_bitcast_fusion.1
  1082.6 2.2 copy.65
  1084.8 3.6 copy.48
  1088.4 3.0 fusion.27
  1091.4 1.4 convolution_bitcast_fusion.3
  1092.9 108.2 %all-reduce.19.cloned.1.call-done = f32[1,512,128]{1,2,0:T(8,128)} async-done(((f32[1,512,128]{1,2,0:T(8,128)}), f32[1,512,128]{1,2,0:T(8,128)}) %all-reduce.19.cloned.1.call-update) | async-done | bytes 262160 | tf_op jit(solution)/shard_map/psum | solution.py:92
  1201.1 1.3 convolution_bitcast_fusion.13
  1203.4 96.5 %all-reduce.21.cloned.1.call-done = f32[4,128,128]{2,1,0:T(8,128)} async-done(((f32[4,128,128]{2,1,0:T(8,128)}), f32[4,128,128]{2,1,0:T(8,128)}) %all-reduce.21.cloned.1.call-update) | async-done | bytes 262160 | tf_op jit(solution)/shard_map/psum | solution.py:103
  1300.2 6.6 fusion.3
  1306.7 1.9 copy.57
  1308.6 34.7 %all-gather.16.cloned.1.call-done = f32[4,2048,128]{2,1,0:T(8,128)} async-done(((f32[4,128,128]{2,1,0:T(8,128)}), f32[4,2048,128]{2,1,0:T(8,128)}) %all-gather.16.cloned.1.call-update) | async-done | bytes 4194320 | tf_op jit(solution)/shard_map/all_gather | solution.py:166
  1343.3 9.6 fusion
  1352.9 3.8 copy.59
  1356.7 1.9 maximum_bitcast_fusion
  1358.6 2.7 copy.66
  1361.3 5.5 copy.51
  1366.8 3.7 fusion.30
  1370.5 1.4 convolution_bitcast_fusion.2
  1372.0 108.6 %all-reduce.23.cloned.1.call-done = f32[1,512,128]{1,2,0:T(8,128)} async-done(((f32[1,512,128]{1,2,0:T(8,128)}), f32[1,512,128]{1,2,0:T(8,128)}) %all-reduce.23.cloned.1.call-update) | async-done | bytes 262160 | tf_op jit(solution)/shard_map/psum | solution.py:92
  1480.6 1.3 convolution_bitcast_fusion.14
  1483.6 95.9 %all-reduce.25.cloned.1.call-done = f32[8,64,128]{2,1,0:T(8,128)} async-done(((f32[8,64,128]{2,1,0:T(8,128)}), f32[8,64,128]{2,1,0:T(8,128)}) %all-reduce.25.cloned.1.call-update) | async-done | bytes 262160 | tf_op jit(solution)/shard_map/psum | solution.py:103
  1580.8 1.7 copy.85
  (112 shorter events, 15.7 us)
Async XLA Ops:
  7.2 270.6 %copy-start = (f32[512,256]{1,0:T(8,128)S(1)}, f32[512,256]{1,0:T(8,128)}, u32[]{:S(2)}) copy-start(f32[512,256]{1,0:T(8,128)} %param.23) | copy-start | bytes 1572868
  7.2 48.1 %all-gather.18.cloned.1.call-start = ((), (), s32[]{:S(2)}) async-start(), calls=%async_computation.15 | async-start | bytes 4456448 | tf_op jit(solution)/shard_map/all_gather | solution.py:26
  9.4 121.8 %reduce-scatter.4.cloned.1.call-start = ((), (), s32[]{:S(2)}) async-start(), calls=%async_computation.3 | async-start | bytes 4456448 | tf_op jit(solution)/shard_map/reduce_scatter | solution.py:65
  60.7 1.0 copy-start.4
  64.3 1.9 copy-start.1
  69.0 158.4 %copy-start.7 = (f32[128,512]{1,0:T(8,128)S(1)}, f32[128,512]{1,0:T(8,128)}, u32[]{:S(2)}) copy-start(f32[128,512]{1,0:T(8,128)} %param.20) | copy-start | bytes 786436
  69.0 160.7 %copy-start.17 = (s32[4,2]{0,1:T(2,128)S(1)}, s32[4,2]{0,1:T(2,128)}, u32[]{:S(2)}) copy-start(s32[4,2]{0,1:T(2,128)} %param.26) | copy-start | bytes 100
  69.0 158.4 %all-reduce.11.cloned.1.call-start = ((), (), s32[]{:S(2)}) async-start(), calls=%async_computation.4 | async-start | bytes 524288 | tf_op jit(solution)/shard_map/psum | solution.py:66
  131.2 140.2 %all-gather.20.cloned.1.call-start = ((), (), s32[]{:S(2)}) async-start(), calls=%async_computation.16 | async-start | bytes 4456448 | tf_op jit(solution)/shard_map/all_gather | solution.py:26
  229.4 112.6 %reduce-scatter.6.cloned.1.call-start = ((), (), s32[]{:S(2)}) async-start(), calls=%async_computation.21 | async-start | bytes 2228224 | tf_op jit(solution)/shard_map/reduce_scatter | solution.py:65
  279.9 1.7 copy-start.2
  283.2 153.1 %copy-start.9 = (f32[128,256]{1,0:T(8,128)S(1)}, f32[128,256]{1,0:T(8,128)}, u32[]{:S(2)}) copy-start(f32[128,256]{1,0:T(8,128)} %param.19) | copy-start | bytes 393220
  283.2 153.1 %copy-start.16 = (f32[2,128,128]{2,1,0:T(8,128)S(1)}, f32[2,128,128]{2,1,0:T(8,128)}, u32[]{:S(2)}) copy-start(f32[2,128,128]{2,1,0:T(8,128)} %param.15) | copy-start | bytes 393220
  283.2 155.0 %copy-start.18 = (s32[2,1]{0,1:T(1,128)S(1)}, s32[2,1]{0,1:T(1,128)}, u32[]{:S(2)}) copy-start(s32[2,1]{0,1:T(1,128)} %param.25) | copy-start | bytes 28
  283.3 153.1 %all-reduce.27.cloned.1.call-start = ((), (), s32[]{:S(2)}) async-start(), calls=%async_computation.19 | async-start | bytes 262144 | tf_op jit(solution)/shard_map/psum | solution.py:66
  342.0 136.1 %all-gather.22.cloned.1.call-start = ((), (), s32[]{:S(2)}) async-start(), calls=%async_computation.17 | async-start | bytes 2228224 | tf_op jit(solution)/shard_map/all_gather | solution.py:26
  438.2 106.7 %reduce-scatter.8.cloned.1.call-start = ((), (), s32[]{:S(2)}) async-start(), calls=%async_computation.22 | async-start | bytes 2228224 | tf_op jit(solution)/shard_map/reduce_scatter | solution.py:65
  480.3 0.9 copy-start.10
  486.4 153.3 %copy-start.6 = (f32[256,256]{1,0:T(8,128)S(1)}, f32[256,256]{1,0:T(8,128)}, u32[]{:S(2)}) copy-start(f32[256,256]{1,0:T(8,128)} %param.18) | copy-start | bytes 786436
  486.4 153.3 %copy-start.15 = (f32[1,256,128]{2,1,0:T(8,128)S(1)}, f32[1,256,128]{2,1,0:T(8,128)}, u32[]{:S(2)}) copy-start(f32[1,256,128]{2,1,0:T(8,128)} %param.14) | copy-start | bytes 393220
  486.4 153.3 %all-reduce.29.cloned.1.call-start = ((), (), s32[]{:S(2)}) async-start(), calls=%async_computation.20 | async-start | bytes 262144 | tf_op jit(solution)/shard_map/psum | solution.py:66
  544.9 136.3 %all-gather.24.cloned.1.call-start = ((), (), s32[]{:S(2)}) async-start(), calls=%async_computation.18 | async-start | bytes 2228224 | tf_op jit(solution)/shard_map/all_gather | solution.py:26
  641.7 134.6 %all-reduce.13.cloned.1.call-start = ((), (), s32[]{:S(2)}) async-start(), calls=%async_computation.5 | async-start | bytes 262144 | tf_op jit(solution)/shard_map/psum | solution.py:103
  684.9 132.3 %all-gather.12.cloned.1.call-start = ((), (), s32[]{:S(2)}) async-start(), calls=%async_computation.6 | async-start | bytes 2228224 | tf_op jit(solution)/shard_map/all_gather | solution.py:166
  776.3 155.4 %all-reduce.15.cloned.1.call-start = ((), (), s32[]{:S(2)}) async-start(), calls=%async_computation.7 | async-start | bytes 262144 | tf_op jit(solution)/shard_map/psum | solution.py:92
  821.4 1.5 copy-start.11
  823.8 205.1 %all-reduce.17.cloned.1.call-start = ((), (), s32[]{:S(2)}) async-start(), calls=%async_computation.8 | async-start | bytes 262144 | tf_op jit(solution)/shard_map/psum | solution.py:103
  935.3 134.6 %all-gather.14.cloned.1.call-start = ((), (), s32[]{:S(2)}) async-start(), calls=%async_computation.9 | async-start | bytes 2228224 | tf_op jit(solution)/shard_map/all_gather | solution.py:166
  1028.9 172.2 %all-reduce.19.cloned.1.call-start = ((), (), s32[]{:S(2)}) async-start(), calls=%async_computation.10 | async-start | bytes 524288 | tf_op jit(solution)/shard_map/psum | solution.py:92
  1092.9 207.1 %all-reduce.21.cloned.1.call-start = ((), (), s32[]{:S(2)}) async-start(), calls=%async_computation.11 | async-start | bytes 524288 | tf_op jit(solution)/shard_map/psum | solution.py:103
  1203.3 140.0 %all-gather.16.cloned.1.call-start = ((), (), s32[]{:S(2)}) async-start(), calls=%async_computation.12 | async-start | bytes 4456448 | tf_op jit(solution)/shard_map/all_gather | solution.py:166
  1299.9 180.7 %all-reduce.23.cloned.1.call-start = ((), (), s32[]{:S(2)}) async-start(), calls=%async_computation.13 | async-start | bytes 524288 | tf_op jit(solution)/shard_map/psum | solution.py:92
  1352.9 3.8 copy-start.3
  1366.7 3.8 copy-start.5
  1366.8 113.9 %copy-start.14 = (f32[64,512]{1,0:T(8,128)S(1)}, f32[64,512]{1,0:T(8,128)}, u32[]{:S(2)}) copy-start(f32[64,512]{1,0:T(8,128)} %param.21) | copy-start | bytes 393220
  1370.5 112.3 %copy-start.12 = (f32[1,256,128]{1,2,0:T(8,128)S(1)}, f32[1,256,128]{1,2,0:T(8,128)}, u32[]{:S(2)}) copy-start(f32[1,256,128]{1,2,0:T(8,128)} %all-reduce.13.cloned.1.call-done) | copy-start | bytes 393220
  1370.5 209.0 %copy-start.13 = (f32[2,128,128]{2,1,0:T(8,128)S(1)}, f32[2,128,128]{2,1,0:T(8,128)}, u32[]{:S(2)}) copy-start(f32[2,128,128]{2,1,0:T(8,128)} %all-reduce.17.cloned.1.call-done) | copy-start | bytes 393220
  1370.5 209.6 %copy-start.8 = (f32[4,128,128]{2,1,0:T(8,128)S(1)}, f32[4,128,128]{2,1,0:T(8,128)}, u32[]{:S(2)}) copy-start(f32[4,128,128]{2,1,0:T(8,128)} %all-reduce.21.cloned.1.call-done) | copy-start | bytes 786436
  1372.0 207.5 %all-reduce.25.cloned.1.call-start = ((), (), s32[]{:S(2)}) async-start(), calls=%async_computation.14 | async-start | bytes 524288 | tf_op jit(solution)/shard_map/psum | solution.py:103
Sparse Core Ops, SparseCore 0:
  10.4 44.8 all-gather.17
  69.1 61.9 reduce-scatter.3
  134.3 93.0 all-reduce.10
  229.6 41.6 all-gather.19
  283.4 58.5 reduce-scatter.5
  345.0 91.3 all-reduce.26
  438.8 39.2 all-gather.21
  486.5 58.3 reduce-scatter.7
  548.1 91.5 all-reduce.28
  642.0 39.2 all-gather.23
  685.1 91.1 all-reduce.12
  778.0 39.2 all-gather.11
  823.9 107.7 all-reduce.14
  935.4 93.4 all-reduce.16
  1030.6 39.2 all-gather.13
  1093.0 108.0 all-reduce.18
  1204.7 95.1 all-reduce.20
  1301.6 41.6 all-gather.15
  1372.1 108.4 all-reduce.22
  1484.2 95.1 all-reduce.24
